TPU v7x, 32 devices: a whole 2x2x4 slice. The times are simulated.
32 devices in a mesh: dp: 8 (over z, x), tensor: 4 (over y, core).
Axes of the slice: x: 2, y: 2, z: 4, core: 2. Of those that a mesh axis runs over, the one named last changes fastest.
Arguments:
- layer_input: bfloat16 [5120, 2304], P(('dp', 'tensor')), may hold values from -6 to 6
- cotangent: bfloat16 [5120, 2304], P(('dp', 'tensor')), may hold values from -6 to 6
- norm_gains: bfloat16 [4, 2304], replicated, may hold values from 0.25 to 1.75
- w_query: bfloat16 [2304, 2048], P('dp', 'tensor'), may hold values from -0.125 to 0.125
- w_key: bfloat16 [2304, 1024], P('dp', 'tensor'), may hold values from -0.125 to 0.125
- w_value: bfloat16 [2304, 1024], P('dp', 'tensor'), may hold values from -0.125 to 0.125
- w_output: bfloat16 [2048, 2304], P('tensor', 'dp'), may hold values from -0.125 to 0.125
- w_gate: bfloat16 [2304, 9216], P('dp', 'tensor'), may hold values from -0.125 to 0.125
- w_up: bfloat16 [2304, 9216], P('dp', 'tensor'), may hold values from -0.125 to 0.125
- w_down: bfloat16 [9216, 2304], P('tensor', 'dp'), may hold values from -0.0625 to 0.0625
- query_shrink: bfloat16 [8, 16, 2304], replicated, may hold values from -0.125 to 0.125
- key_shrink: bfloat16 [8, 16, 2304], replicated, may hold values from -0.125 to 0.125
- value_shrink: bfloat16 [8, 16, 2304], replicated, may hold values from -0.125 to 0.125
- output_shrink: bfloat16 [8, 16, 2048], P(None, None, 'tensor'), may hold values from -0.125 to 0.125
- gate_shrink: bfloat16 [8, 16, 2304], replicated, may hold values from -0.125 to 0.125
- up_shrink: bfloat16 [8, 16, 2304], replicated, may hold values from -0.125 to 0.125
- down_shrink: bfloat16 [8, 16, 9216], P(None, None, 'tensor'), may hold values from -0.0625 to 0.0625
- query_expand: bfloat16 [8, 16, 2048], P(None, None, 'tensor'), may hold values from -0.75 to 0.75
- key_expand: bfloat16 [8, 16, 1024], P(None, None, 'tensor'), may hold values from -0.75 to 0.75
- value_expand: bfloat16 [8, 16, 1024], P(None, None, 'tensor'), may hold values from -0.75 to 0.75
- output_expand: bfloat16 [8, 16, 2304], replicated, may hold values from -0.75 to 0.75
- gate_expand: bfloat16 [8, 16, 9216], P(None, None, 'tensor'), may hold values from -0.75 to 0.75
- up_expand: bfloat16 [8, 16, 9216], P(None, None, 'tensor'), may hold values from -0.75 to 0.75
- down_expand: bfloat16 [8, 16, 2304], replicated, may hold values from -0.75 to 0.75
- adapter_ids: int32 [8], P('dp'), may hold values from 0 to 7
- parent_segments: int32 [8, 13], P('dp'), may hold values from 0 to 4, as said below
- segment_ids: int32 [5120], P('dp'), may hold values from 0 to 12, as said below
Outputs:
- layer_output: bfloat16 [5120, 2304], P(('dp', 'tensor'))
- input_grad: float32 [5120, 2304], P(('dp', 'tensor'))
- shrink_query: float32 [8, 16, 2304], replicated
- shrink_key: float32 [8, 16, 2304], replicated
- shrink_value: float32 [8, 16, 2304], replicated
- shrink_output: float32 [8, 16, 2048], P(None, None, 'tensor')
- shrink_gate: float32 [8, 16, 2304], replicated
- shrink_up: float32 [8, 16, 2304], replicated
- shrink_down: float32 [8, 16, 9216], P(None, None, 'tensor')
- expand_query: float32 [8, 16, 2048], P(None, None, 'tensor')
- expand_key: float32 [8, 16, 1024], P(None, None, 'tensor')
- expand_value: float32 [8, 16, 1024], P(None, None, 'tensor')
- expand_output: float32 [8, 16, 2304], replicated
- expand_gate: float32 [8, 16, 9216], P(None, None, 'tensor')
- expand_up: float32 [8, 16, 9216], P(None, None, 'tensor')
- expand_down: float32 [8, 16, 2304], replicated
Inputs may be any that keep to these rules, and one draw needn't show every extreme that they name: `parent_segments`: in each tree, segment 0 is the trunk and is its own parent; segments 1 to 4 have parent 0; each of the other segments has a branch (1 to 4) as parent, and every branch is the parent of exactly 2 of them. `segment_ids`: the first 256 tokens of each tree are segment 0; the rest are 12 contiguous runs of 32 tokens, one run for each other segment, in any order.
All inputs are finite; a program needn't handle non-finite values.
Results may differ from a plain program's by a relative error of at most 0.028.
Values may be sent and summed in bfloat16 or wider, within the bound.
No kernel may reach another device: no remote copies, remote signals or barrier semaphores. Data moves between devices by JAX's collectives and lax.ppermute only.
A program may use at most 256 MiB of HBM per device.

v0:
```python
import math
import jax
import jax.numpy as jnp
from jax import lax
from jax.sharding import PartitionSpec as P

HEAD_WIDTH = 256
ADAPTERS = 8


def rms_scale(value_rows, gain_row):
    inverse = lax.rsqrt(jnp.mean(value_rows * value_rows, axis=-1, keepdims=True) + 1e-06)
    return value_rows * inverse * gain_row


def rms_back(value_rows, gain_row, upstream):
    inverse = lax.rsqrt(jnp.mean(value_rows * value_rows, axis=-1, keepdims=True) + 1e-06)
    scaled = gain_row * upstream
    return inverse * scaled - value_rows * (inverse * inverse * inverse) * jnp.mean(
        value_rows * scaled, axis=-1, keepdims=True
    )


def pick_from(lookup, indices, labels):
    return jnp.sum(jnp.where(indices[:, None] == labels[None, :], lookup[None, :], 0), axis=1)


def tree_tables(segments, parents):
    count_seg = parents.shape[0]
    sequence_length = segments.shape[0]
    labels = jnp.arange(count_seg, dtype=jnp.int32)
    places = jnp.arange(sequence_length, dtype=jnp.int32)
    member = segments[None, :] == labels[:, None]
    starts = jnp.min(jnp.where(member, places[None, :], sequence_length), axis=1)
    counts = jnp.sum(member.astype(jnp.int32), axis=1)
    grands = pick_from(parents, parents, labels)
    offsets = jnp.where(parents != labels, pick_from(counts, parents, labels), 0) + jnp.where(
        grands != parents, pick_from(counts, grands, labels), 0
    )
    tok_start = pick_from(starts, segments, labels)
    tok_offset = pick_from(offsets, segments, labels)
    tok_parent = pick_from(parents, segments, labels)
    tok_grand = pick_from(grands, segments, labels)
    positions = (places - tok_start + tok_offset).astype(jnp.float32)
    same_seg = (segments[None, :] == segments[:, None]) & (places[None, :] <= places[:, None])
    from_parent = (segments[None, :] == tok_parent[:, None]) & (tok_parent != segments)[:, None]
    from_grand = (segments[None, :] == tok_grand[:, None]) & (tok_grand != tok_parent)[:, None]
    visible = same_seg | from_parent | from_grand
    inv_freq = jnp.exp(
        jnp.arange(HEAD_WIDTH // 2, dtype=jnp.float32) * (-2.0 * math.log(10000.0) / HEAD_WIDTH)
    )
    angles = positions[:, None] * inv_freq[None, :]
    return (visible, jnp.cos(angles), jnp.sin(angles))


def apply_rotary(value_rows, cos_rows, sin_rows):
    half_size = value_rows.shape[-1] // 2
    front_half = value_rows[..., :half_size]
    back_half = value_rows[..., half_size:]
    return jnp.concatenate(
        [
            front_half * cos_rows - back_half * sin_rows,
            back_half * cos_rows + front_half * sin_rows,
        ],
        axis=-1,
    )


def rotate_back(value_rows, cos_rows, sin_rows):
    half_size = value_rows.shape[-1] // 2
    front_half = value_rows[..., :half_size]
    back_half = value_rows[..., half_size:]
    return jnp.concatenate(
        [
            front_half * cos_rows + back_half * sin_rows,
            back_half * cos_rows - front_half * sin_rows,
        ],
        axis=-1,
    )


def product(former, latter):
    return jnp.dot(former, latter, preferred_element_type=jnp.float32)


def select(onehot, stacked):
    return jnp.einsum("e,erc->rc", onehot, stacked, preferred_element_type=jnp.float32).astype(
        jnp.bfloat16
    )


def project(inputs, weight, shrink, expand):
    inner_rank = jnp.einsum("li,ri->lr", inputs, shrink, preferred_element_type=jnp.float32)
    return (product(inputs, weight) + product(inner_rank, expand.astype(jnp.float32)), inner_rank)


def project_back(inputs, inner_rank, upstream, weight, shrink, expand):
    grad_expand = jnp.einsum("lr,lo->ro", inner_rank, upstream, preferred_element_type=jnp.float32)
    grad_inner = jnp.einsum("lo,ro->lr", upstream, expand, preferred_element_type=jnp.float32)
    grad_shrink = jnp.einsum("lr,li->ri", grad_inner, inputs, preferred_element_type=jnp.float32)
    grad_inputs = jnp.einsum(
        "lo,io->li", upstream, weight, preferred_element_type=jnp.float32
    ) + product(grad_inner, shrink.astype(jnp.float32))
    return (grad_inputs, grad_shrink, grad_expand)


def score_block(query_rows, rotated_keys, visible):
    scores = jnp.einsum(
        "qngd,knd->ngqk", query_rows, rotated_keys, preferred_element_type=jnp.float32
    )
    bounded = jnp.tanh(scores / 50.0)
    masked = jnp.where(visible[None, None], 50.0 * bounded, -1e30)
    return (bounded, masked)


def activate(gate_in, up_in):
    return jax.nn.gelu(gate_in, approximate=True) * up_in


def on_device(
    layer_input,
    cotangent,
    norm_gains,
    w_query,
    w_key,
    w_value,
    w_output,
    w_gate,
    w_up,
    w_down,
    query_shrink,
    key_shrink,
    value_shrink,
    output_shrink,
    gate_shrink,
    up_shrink,
    down_shrink,
    query_expand,
    key_expand,
    value_expand,
    output_expand,
    gate_expand,
    up_expand,
    down_expand,
    adapter_ids,
    parent_segments,
    segment_ids,
):
    norm_gain = norm_gains.astype(jnp.float32)
    w_query, w_key, w_value, w_output, w_gate, w_up, w_down = (
        lax.all_gather(w_query, "dp", axis=0, tiled=True),
        lax.all_gather(w_key, "dp", axis=0, tiled=True),
        lax.all_gather(w_value, "dp", axis=0, tiled=True),
        lax.all_gather(w_output, "dp", axis=1, tiled=True),
        lax.all_gather(w_gate, "dp", axis=0, tiled=True),
        lax.all_gather(w_up, "dp", axis=0, tiled=True),
        lax.all_gather(w_down, "dp", axis=1, tiled=True),
    )
    labels = jnp.arange(ADAPTERS, dtype=jnp.int32)
    onehot = (labels == adapter_ids[0]).astype(jnp.bfloat16)
    chosen = [
        select(onehot, stacked)
        for stacked in (
            query_shrink,
            key_shrink,
            value_shrink,
            output_shrink,
            gate_shrink,
            up_shrink,
            down_shrink,
            query_expand,
            key_expand,
            value_expand,
            output_expand,
            gate_expand,
            up_expand,
            down_expand,
        )
    ]
    s_query, s_key, s_value, s_output, s_gate, s_up, s_down = chosen[:7]
    e_query, e_key, e_value, e_output, e_gate, e_up, e_down = chosen[7:]
    visible, cos_rows, sin_rows = tree_tables(segment_ids, parent_segments[0])
    cosine_per_head = cos_rows[:, None, :]
    sine_per_head = sin_rows[:, None, :]
    own_rows = layer_input.astype(jnp.float32)
    normed = rms_scale(own_rows, norm_gain[0]).astype(jnp.bfloat16)
    normed_all = lax.all_gather(normed, "tensor", axis=0, tiled=True)
    sequence_length = normed_all.shape[0]
    query_pre, query_inner = project(normed_all, w_query, s_query, e_query)
    key_before_rotation, key_inner = project(normed_all, w_key, s_key, e_key)
    value_projected, value_inner = project(normed_all, w_value, s_value, e_value)
    heads_q = query_pre.shape[1] // HEAD_WIDTH
    heads_kv = key_before_rotation.shape[1] // HEAD_WIDTH
    head_groups = heads_q // heads_kv
    query_rows = (
        (
            apply_rotary(
                query_pre.reshape(sequence_length, heads_q, HEAD_WIDTH),
                cosine_per_head,
                sine_per_head,
            )
            * HEAD_WIDTH ** (-0.5)
        )
        .astype(jnp.bfloat16)
        .reshape(sequence_length, heads_kv, head_groups, HEAD_WIDTH)
    )
    rotated_keys = apply_rotary(
        key_before_rotation.reshape(sequence_length, heads_kv, HEAD_WIDTH),
        cosine_per_head,
        sine_per_head,
    ).astype(jnp.bfloat16)
    value_rows = value_projected.astype(jnp.bfloat16).reshape(sequence_length, heads_kv, HEAD_WIDTH)
    bounded, masked = score_block(query_rows, rotated_keys, visible)
    row_max = jnp.max(masked, axis=-1, keepdims=True)
    exponent = jnp.exp(masked - row_max)
    row_total = jnp.sum(exponent, axis=-1, keepdims=True)
    log_total = row_max + jnp.log(row_total)
    probs_low = (exponent / row_total).astype(jnp.bfloat16)
    mixed_heads = (
        jnp.einsum("ngqk,knd->qngd", probs_low, value_rows, preferred_element_type=jnp.float32)
        .reshape(sequence_length, heads_q * HEAD_WIDTH)
        .astype(jnp.bfloat16)
    )
    attn_part, output_inner = project(mixed_heads, w_output, s_output, e_output)
    attended = lax.psum_scatter(
        attn_part.astype(jnp.bfloat16), "tensor", scatter_dimension=0, tiled=True
    ).astype(jnp.float32)
    residual = own_rows + rms_scale(attended, norm_gain[1])
    normed_ffn = rms_scale(residual, norm_gain[2]).astype(jnp.bfloat16)
    ffn_rows = lax.all_gather(normed_ffn, "tensor", axis=0, tiled=True)
    gate_pre, gate_inner = project(ffn_rows, w_gate, s_gate, e_gate)
    up_pre, up_inner = project(ffn_rows, w_up, s_up, e_up)
    hidden_full, act_back = jax.vjp(activate, gate_pre, up_pre)
    hidden = hidden_full.astype(jnp.bfloat16)
    ffn_part, down_inner = project(hidden, w_down, s_down, e_down)
    ffn_out = lax.psum_scatter(
        ffn_part.astype(jnp.bfloat16), "tensor", scatter_dimension=0, tiled=True
    ).astype(jnp.float32)
    layer_output = (residual + rms_scale(ffn_out, norm_gain[3])).astype(jnp.bfloat16)
    grad_out = cotangent.astype(jnp.float32)
    grad_ffn = rms_back(ffn_out, norm_gain[3], grad_out).astype(jnp.bfloat16)
    grad_ffn_all = lax.all_gather(grad_ffn, "tensor", axis=0, tiled=True)
    down_back = project_back(hidden, down_inner, grad_ffn_all, w_down, s_down, e_down)
    grad_gate, grad_up = act_back(down_back[0])
    grad_gate = grad_gate.astype(jnp.bfloat16)
    grad_up = grad_up.astype(jnp.bfloat16)
    gate_back = project_back(ffn_rows, gate_inner, grad_gate, w_gate, s_gate, e_gate)
    up_back = project_back(ffn_rows, up_inner, grad_up, w_up, s_up, e_up)
    grad_normed_ffn = lax.psum_scatter(
        (gate_back[0] + up_back[0]).astype(jnp.bfloat16), "tensor", scatter_dimension=0, tiled=True
    ).astype(jnp.float32)
    grad_resid = grad_out + rms_back(residual, norm_gain[2], grad_normed_ffn)
    grad_attn = rms_back(attended, norm_gain[1], grad_resid).astype(jnp.bfloat16)
    grad_attn_all = lax.all_gather(grad_attn, "tensor", axis=0, tiled=True)
    output_back = project_back(
        mixed_heads, output_inner, grad_attn_all, w_output, s_output, e_output
    )
    grad_mixed = (
        output_back[0]
        .astype(jnp.bfloat16)
        .reshape(sequence_length, heads_kv, head_groups, HEAD_WIDTH)
    )
    bounded, masked = score_block(query_rows, rotated_keys, visible)
    attn_probs = jnp.exp(masked - log_total)
    probs_low = attn_probs.astype(jnp.bfloat16)
    grad_values = (
        jnp.einsum("ngqk,qngd->knd", probs_low, grad_mixed, preferred_element_type=jnp.float32)
        .reshape(sequence_length, heads_kv * HEAD_WIDTH)
        .astype(jnp.bfloat16)
    )
    grad_probs = jnp.einsum(
        "qngd,knd->ngqk", grad_mixed, value_rows, preferred_element_type=jnp.float32
    )
    grad_capped = attn_probs * (
        grad_probs - jnp.sum(attn_probs * grad_probs, axis=-1, keepdims=True)
    )
    grad_scores = (grad_capped * (1.0 - bounded * bounded)).astype(jnp.bfloat16)
    grad_queries = jnp.einsum(
        "ngqk,knd->qngd", grad_scores, rotated_keys, preferred_element_type=jnp.float32
    ).reshape(sequence_length, heads_q, HEAD_WIDTH)
    grad_keys = jnp.einsum(
        "ngqk,qngd->knd", grad_scores, query_rows, preferred_element_type=jnp.float32
    )
    grad_qpre = (
        rotate_back(grad_queries * HEAD_WIDTH ** (-0.5), cosine_per_head, sine_per_head)
        .reshape(sequence_length, heads_q * HEAD_WIDTH)
        .astype(jnp.bfloat16)
    )
    grad_kpre = (
        rotate_back(grad_keys, cosine_per_head, sine_per_head)
        .reshape(sequence_length, heads_kv * HEAD_WIDTH)
        .astype(jnp.bfloat16)
    )
    query_back = project_back(normed_all, query_inner, grad_qpre, w_query, s_query, e_query)
    key_back = project_back(normed_all, key_inner, grad_kpre, w_key, s_key, e_key)
    value_back = project_back(normed_all, value_inner, grad_values, w_value, s_value, e_value)
    grad_normed = lax.psum_scatter(
        (query_back[0] + key_back[0] + value_back[0]).astype(jnp.bfloat16),
        "tensor",
        scatter_dimension=0,
        tiled=True,
    ).astype(jnp.float32)
    input_grad = grad_resid + rms_back(own_rows, norm_gain[0], grad_normed)
    hot_rows = onehot.astype(jnp.float32)[:, None, None]
    split_sums = (
        lax.psum((hot_rows * query_back[2][None]).astype(jnp.bfloat16), "dp").astype(jnp.float32),
        lax.psum((hot_rows * key_back[2][None]).astype(jnp.bfloat16), "dp").astype(jnp.float32),
        lax.psum((hot_rows * value_back[2][None]).astype(jnp.bfloat16), "dp").astype(jnp.float32),
        lax.psum((hot_rows * output_back[1][None]).astype(jnp.bfloat16), "dp").astype(jnp.float32),
        lax.psum((hot_rows * gate_back[2][None]).astype(jnp.bfloat16), "dp").astype(jnp.float32),
        lax.psum((hot_rows * up_back[2][None]).astype(jnp.bfloat16), "dp").astype(jnp.float32),
        lax.psum((hot_rows * down_back[1][None]).astype(jnp.bfloat16), "dp").astype(jnp.float32),
    )
    shared_sums = lax.psum(
        (
            hot_rows * query_back[1][None],
            hot_rows * key_back[1][None],
            hot_rows * value_back[1][None],
            hot_rows * output_back[2][None],
            hot_rows * gate_back[1][None],
            hot_rows * up_back[1][None],
            hot_rows * down_back[2][None],
        ),
        ("dp", "tensor"),
    )
    return (
        layer_output,
        input_grad,
        shared_sums[0],
        shared_sums[1],
        shared_sums[2],
        split_sums[3],
        shared_sums[4],
        shared_sums[5],
        split_sums[6],
        split_sums[0],
        split_sums[1],
        split_sums[2],
        shared_sums[3],
        split_sums[4],
        split_sums[5],
        shared_sums[6],
    )


def solution(mesh):
    placed = (
        P(("dp", "tensor"), None),
        P(("dp", "tensor"), None),
        P(),
        P("dp", "tensor"),
        P("dp", "tensor"),
        P("dp", "tensor"),
        P("tensor", "dp"),
        P("dp", "tensor"),
        P("dp", "tensor"),
        P("tensor", "dp"),
        P(),
        P(),
        P(),
        P(None, None, "tensor"),
        P(),
        P(),
        P(None, None, "tensor"),
        P(None, None, "tensor"),
        P(None, None, "tensor"),
        P(None, None, "tensor"),
        P(),
        P(None, None, "tensor"),
        P(None, None, "tensor"),
        P(),
        P("dp"),
        P("dp", None),
        P("dp"),
    )
    return jax.shard_map(
        on_device,
        mesh=mesh,
        in_specs=placed,
        out_specs=(
            P(("dp", "tensor"), None),
            P(("dp", "tensor"), None),
            P(),
            P(),
            P(),
            P(None, None, "tensor"),
            P(),
            P(),
            P(None, None, "tensor"),
            P(None, None, "tensor"),
            P(None, None, "tensor"),
            P(None, None, "tensor"),
            P(),
            P(None, None, "tensor"),
            P(None, None, "tensor"),
            P(),
        ),
        check_vma=False,
    )
```

profile of v0, /device:TPU:0, one launch (start us, length us, event | category | flops | bytes accessed | tf_op | source)
XLA Modules:
  0.0 1369.6 jit_solution(2153370588222020406)
XLA Ops:
  26.4 17.0 %all-gather.12.cloned.1.call-done = bf16[640,2304]{1,0:T(8,128)(2,1)} async-done(((bf16[160,2304]{1,0:T(8,128)(2,1)}), bf16[640,2304]{1,0:T(8,128)(2,1)}) %all-gather.12.cloned.1.call-update) | async-done | bytes 2949136 | tf_op jit(solution)/shard_map/all_gather | solution.py:187
  43.4 2.8 fusion.129
  46.2 51.4 %all-gather.18.cloned.1.call-done = bf16[2304,512]{1,0:T(8,128)(2,1)} async-done(((bf16[288,512]{1,0:T(8,128)(2,1)}), bf16[2304,512]{1,0:T(8,128)(2,1)}) %all-gather.18.cloned.1.call-update) | async-done | bytes 2359312 | tf_op jit(solution)/shard_map/all_gather | solution.py:151
  97.7 3.7 fusion.192
  109.0 30.4 %all-gather.16.cloned.1.call-done = bf16[2304,256]{1,0:T(8,128)(2,1)} async-done(((bf16[288,256]{1,0:T(8,128)(2,1)}), bf16[2304,256]{1,0:T(8,128)(2,1)}) %all-gather.16.cloned.1.call-update) | async-done | bytes 1179664 | tf_op jit(solution)/shard_map/all_gather | solution.py:152
  139.5 2.4 fusion.191
  143.9 37.5 %all-gather.14.cloned.1.call-done = bf16[2304,256]{1,0:T(8,128)(2,1)} async-done(((bf16[288,256]{1,0:T(8,128)(2,1)}), bf16[2304,256]{1,0:T(8,128)(2,1)}) %all-gather.14.cloned.1.call-update) | async-done | bytes 1179664 | tf_op jit(solution)/shard_map/all_gather | solution.py:153
  190.3 44.0 %all-gather.20.cloned.1.call-done = bf16[512,2304]{0,1:T(8,128)(2,1)} async-done(((bf16[512,288]{0,1:T(8,128)(2,1)}), bf16[512,2304]{0,1:T(8,128)(2,1)}) %all-gather.20.cloned.1.call-update) | async-done | bytes 2359312 | tf_op jit(solution)/shard_map/all_gather | solution.py:154
  234.3 3.4 fusion.193
  237.7 2.6 add_convert_fusion.3
  240.4 35.4 %reduce-scatter.5.cloned.1.call-done = bf16[160,2304]{1,0:T(8,128)(2,1)} async-done(((bf16[640,2304]{1,0:T(8,128)(2,1)}), bf16[160,2304]{1,0:T(8,128)(2,1)}) %reduce-scatter.5.cloned.1.call-update) | async-done | bytes 737296 | tf_op jit(solution)/shard_map/reduce_scatter | solution.py:225
  280.0 2.5 multiply_convert_fusion.2
  287.9 22.2 %all-gather.22.cloned.1.call-done = bf16[640,2304]{1,0:T(8,128)(2,1)} async-done(((bf16[160,2304]{1,0:T(8,128)(2,1)}), bf16[640,2304]{1,0:T(8,128)(2,1)}) %all-gather.22.cloned.1.call-update) | async-done | bytes 2949136 | tf_op jit(solution)/shard_map/all_gather | solution.py:230
  310.1 3.5 fusion.134
  313.5 2.4 fusion.132
  315.9 149.0 %all-gather.24.cloned.1.call-done = bf16[2304,2304]{1,0:T(8,128)(2,1)} async-done(((bf16[288,2304]{1,0:T(8,128)(2,1)}), bf16[2304,2304]{1,0:T(8,128)(2,1)}) %all-gather.24.cloned.1.call-update) | async-done | bytes 10616848 | tf_op jit(solution)/shard_map/all_gather | solution.py:155
  465.0 9.6 fusion.194
  474.5 3.4 convolution_add_fusion.2
  478.0 140.1 %all-gather.26.cloned.1.call-done = bf16[2304,2304]{1,0:T(8,128)(2,1)} async-done(((bf16[288,2304]{1,0:T(8,128)(2,1)}), bf16[2304,2304]{1,0:T(8,128)(2,1)}) %all-gather.26.cloned.1.call-update) | async-done | bytes 10616848 | tf_op jit(solution)/shard_map/all_gather | solution.py:156
  618.0 9.5 fusion.195
  627.6 4.2 multiply_convert_fusion.1
  634.9 136.1 %all-gather.28.cloned.1.call-done = bf16[2304,2304]{0,1:T(8,128)(2,1)} async-done(((bf16[2304,288]{0,1:T(8,128)(2,1)}), bf16[2304,2304]{0,1:T(8,128)(2,1)}) %all-gather.28.cloned.1.call-update) | async-done | bytes 10616848 | tf_op jit(solution)/shard_map/all_gather | solution.py:157
  771.0 10.4 fusion.196
  781.4 2.6 add_convert_fusion.2
  784.1 35.0 %reduce-scatter.7.cloned.1.call-done = bf16[160,2304]{1,0:T(8,128)(2,1)} async-done(((bf16[640,2304]{1,0:T(8,128)(2,1)}), bf16[160,2304]{1,0:T(8,128)(2,1)}) %reduce-scatter.7.cloned.1.call-update) | async-done | bytes 737296 | tf_op jit(solution)/shard_map/reduce_scatter | solution.py:236
  820.9 2.6 fusion.27
  823.6 27.5 %all-gather.30.cloned.1.call-done = bf16[640,2304]{1,0:T(8,128)(2,1)} async-done(((bf16[160,2304]{1,0:T(8,128)(2,1)}), bf16[640,2304]{1,0:T(8,128)(2,1)}) %all-gather.30.cloned.1.call-update) | async-done | bytes 2949136 | tf_op jit(solution)/shard_map/all_gather | solution.py:242
  851.1 11.4 fusion.197
  863.5 8.0 fusion.6
  874.5 12.2 fusion.199
  886.7 12.2 fusion.198
  898.8 7.3 add_convert_fusion.1
  906.7 36.3 %reduce-scatter.9.cloned.1.call-done = bf16[160,2304]{1,0:T(8,128)(2,1)} async-done(((bf16[640,2304]{1,0:T(8,128)(2,1)}), bf16[160,2304]{1,0:T(8,128)(2,1)}) %reduce-scatter.9.cloned.1.call-update) | async-done | bytes 737296 | tf_op jit(solution)/shard_map/reduce_scatter | solution.py:249
  945.2 4.2 fusion.33
  952.6 3.3 fusion.208
  961.7 17.8 %all-gather.32.cloned.1.call-done = bf16[640,2304]{1,0:T(8,128)(2,1)} async-done(((bf16[160,2304]{1,0:T(8,128)(2,1)}), bf16[640,2304]{1,0:T(8,128)(2,1)}) %all-gather.32.cloned.1.call-update) | async-done | bytes 2949136 | tf_op jit(solution)/shard_map/all_gather | solution.py:254
  979.5 2.8 fusion.130
  982.7 3.8 fusion.200
  1003.6 3.6 fusion.128
  1007.2 3.4 fusion.126
  1010.6 3.5 fusion.124
  1017.9 4.0 multiply_convert_fusion.3
  1026.7 10.2 add_convert_fusion
  1037.5 90.8 %all-reduce.7.cloned.1.call-done = (bf16[8,16,512]{2,1,0:T(8,128)(2,1)}, bf16[8,16,2304]{2,1,0:T(8,128)(2,1)}, bf16[8,16,512]{2,1,0:T(8,128)(2,1)}, bf16[8,16,25...) async-done(((bf16[8,16,512]{2,1,0:T(8,128)(2,1)}, bf16[8,16,2304]{2,1,0:T(8,128)(2,1)}, ...) | async-done | bytes 2162704 | tf_op jit(solution)/shard_map/psum | solution.py:309
  1139.2 27.3 %reduce-scatter.11.cloned.1.call-done = bf16[160,2304]{1,0:T(8,128)(2,1)} async-done(((bf16[640,2304]{1,0:T(8,128)(2,1)}), bf16[160,2304]{1,0:T(8,128)(2,1)}) %reduce-scatter.11.cloned.1.call-update) | async-done | bytes 737296 | tf_op jit(solution)/shard_map/reduce_scatter | solution.py:297
  1168.0 2.7 fusion.45
  1170.7 183.6 %all-reduce.5.cloned.1.call-done = (f32[8,16,2304]{2,1,0:T(8,128)}, f32[8,16,2304]{2,1,0:T(8,128)}, f32[8,16,2304]{2,1,0:T(8,128)}, f32[8,16,2304]{2,1,0:T(8,128...) async-done(((f32[8,16,2304]{2,1,0:T(8,128)}, f32[8,16,2304]{2,1,0:T(8,128)}, f32[8,16,2304]{2,1,0:T(8,128)}, f32[8,16,2304]{2,1,0:T(8,128)}, ...) | async-done | bytes 8257552 | tf_op jit(solution)/shard_map/psum | solution.py:314
  1354.2 2.5 copy.208
  (422 shorter events, 111.0 us)
Async XLA Ops:
  7.3 14.0 %copy-start.58 = (bf16[8,16,2304]{2,1,0:T(8,128)(2,1)S(1)}, bf16[8,16,2304]{2,1,0:T(8,128)(2,1)}, u32[]{:S(2)}) copy-start(bf16[8,16,2304]{2,1,0:T(8,128)(2,1)} %param.38) | copy-start | bytes 1769476
  7.3 15.0 %copy-start.59 = (bf16[8,16,2304]{2,1,0:T(8,128)(2,1)S(1)}, bf16[8,16,2304]{2,1,0:T(8,128)(2,1)}, u32[]{:S(2)}) copy-start(bf16[8,16,2304]{2,1,0:T(8,128)(2,1)} %param.39) | copy-start | bytes 1769476
  7.3 36.1 %all-gather.12.cloned.1.call-start = ((), (), s32[]{:S(2)}) async-start(), calls=%async_computation.4 | async-start | bytes 3686400 | tf_op jit(solution)/shard_map/all_gather | solution.py:187
  10.8 269.1 %copy-start.78 = (f32[2304]{0:T(1024)}, f32[2304]{0:T(1024)S(1)}, u32[]{:S(2)}) copy-start(f32[2304]{0:T(1024)S(1)} %get-tuple-element.20) | copy-start | bytes 27652
  13.1 84.6 %all-gather.18.cloned.1.call-start = ((), (), s32[]{:S(2)}) async-start(), calls=%async_computation.7 | async-start | bytes 2654208 | tf_op jit(solution)/shard_map/all_gather | solution.py:151
  13.9 125.6 %all-gather.16.cloned.1.call-start = ((), (), s32[]{:S(2)}) async-start(), calls=%async_computation.6 | async-start | bytes 1327104 | tf_op jit(solution)/shard_map/all_gather | solution.py:152
  14.6 166.8 %all-gather.14.cloned.1.call-start = ((), (), s32[]{:S(2)}) async-start(), calls=%async_computation.5 | async-start | bytes 1327104 | tf_op jit(solution)/shard_map/all_gather | solution.py:153
  15.2 219.1 %all-gather.20.cloned.1.call-start = ((), (), s32[]{:S(2)}) async-start(), calls=%async_computation.8 | async-start | bytes 2654208 | tf_op jit(solution)/shard_map/all_gather | solution.py:154
  15.8 260.0 %reduce-scatter.5.cloned.1.call-start = ((), (), s32[]{:S(2)}) async-start(), calls=%async_computation.9 | async-start | bytes 3686400 | tf_op jit(solution)/shard_map/reduce_scatter | solution.py:225
  17.1 166.9 %copy-start.112 = (f32[640]{0:T(1024)}, f32[640]{0:T(1024)S(1)}, u32[]{:S(2)}) copy-start(f32[640]{0:T(1024)S(1)} %add_convert_fusion.5) | copy-start | bytes 7684
  22.6 120.5 %copy-start.73 = (bf16[1,16,2304]{2,0,1:T(2,128)(2,1)}, bf16[1,16,2304]{2,0,1:T(2,128)(2,1)S(1)}, u32[]{:S(2)}) copy-start(bf16[1,16,2304]{2,0,1:T(2,128)(2,1)S(1)} %fusion.92) | copy-start | bytes 221188
  24.3 164.2 %copy-start.24 = (pred[640,640]{0,1:T(8,128)(4,1)}, pred[640,640]{0,1:T(8,128)(4,1)S(1)}, u32[]{:S(2)}) copy-start(pred[640,640]{0,1:T(8,128)(4,1)S(1)} %fusion.25) | copy-start | bytes 1228804
  43.4 54.3 %copy-start.2 = (bf16[640,2304]{1,0:T(8,128)(2,1)S(1)}, bf16[640,2304]{1,0:T(8,128)(2,1)}, u32[]{:S(2)}) copy-start(bf16[640,2304]{1,0:T(8,128)(2,1)} %all-gather.12.cloned.1.call-done) | copy-start | bytes 8847364
  46.2 55.2 %copy-start.92 = (bf16[640,16]{0,1:T(8,128)(2,1)}, bf16[640,16]{0,1:T(8,128)(2,1)S(1)}, u32[]{:S(2)}) copy-start(bf16[640,16]{0,1:T(8,128)(2,1)S(1)} %fusion.129) | copy-start | bytes 61444
  109.0 32.9 %copy-start.103 = (bf16[640,16]{0,1:T(8,128)(2,1)}, bf16[640,16]{0,1:T(8,128)(2,1)S(1)}, u32[]{:S(2)}) copy-start(bf16[640,16]{0,1:T(8,128)(2,1)S(1)} %fusion.127) | copy-start | bytes 61444
  143.9 39.8 %copy-start.90 = (bf16[640,16]{0,1:T(8,128)(2,1)}, bf16[640,16]{0,1:T(8,128)(2,1)S(1)}, u32[]{:S(2)}) copy-start(bf16[640,16]{0,1:T(8,128)(2,1)S(1)} %fusion.125) | copy-start | bytes 61444
  143.9 39.9 %copy-start.114 = (bf16[1,16,256]{2,0,1:T(2,128)(2,1)S(1)}, bf16[1,16,256]{2,0,1:T(2,128)(2,1)}, u32[]{:S(2)}) copy-start(bf16[1,16,256]{2,0,1:T(2,128)(2,1)} %fusion.122) | copy-start | bytes 24580
  143.9 40.2 %copy-start.135 = (f32[128]{0:T(128)S(1)}, f32[128]{0:T(128)}, u32[]{:S(2)}) copy-start(f32[128]{0:T(128)} %copy-done.134) | copy-start | bytes 1540
  190.0 47.7 %copy-start.22 = (bf16[256,2,640]{2,0,1:T(8,128)(2,1)}, bf16[256,2,640]{2,0,1:T(8,128)(2,1)S(1)}, u32[]{:S(2)}) copy-start(bf16[256,2,640]{2,0,1:T(8,128)(2,1)S(1)} %fusion.54) | copy-start | bytes 1966084
  190.3 47.5 %copy-start.99 = (bf16[640,16]{0,1:T(8,128)(2,1)}, bf16[640,16]{0,1:T(8,128)(2,1)S(1)}, u32[]{:S(2)}) copy-start(bf16[640,16]{0,1:T(8,128)(2,1)S(1)} %fusion.141) | copy-start | bytes 61444
  190.3 47.5 %copy-start.54 = (bf16[1,16,2304]{2,0,1:T(2,128)(2,1)S(1)}, bf16[1,16,2304]{2,0,1:T(2,128)(2,1)}, u32[]{:S(2)}) copy-start(bf16[1,16,2304]{2,0,1:T(2,128)(2,1)} %fusion.86) | copy-start | bytes 221188
  240.3 37.4 %copy-start.5 = (bf16[160,2304]{1,0:T(8,128)(2,1)S(1)}, bf16[160,2304]{1,0:T(8,128)(2,1)}, u32[]{:S(2)}) copy-start(bf16[160,2304]{1,0:T(8,128)(2,1)} %param.27) | copy-start | bytes 2211844
  240.3 39.6 %copy-start.97 = (f32[2304]{0:T(1024)S(1)}, f32[2304]{0:T(1024)}, u32[]{:S(2)}) copy-start(f32[2304]{0:T(1024)} %get-tuple-element.19) | copy-start | bytes 27652
  240.4 69.7 %all-gather.22.cloned.1.call-start = ((), (), s32[]{:S(2)}) async-start(), calls=%async_computation.10 | async-start | bytes 3686400 | tf_op jit(solution)/shard_map/all_gather | solution.py:230
  282.5 182.5 %all-gather.24.cloned.1.call-start = ((), (), s32[]{:S(2)}) async-start(), calls=%async_computation.11 | async-start | bytes 11943936 | tf_op jit(solution)/shard_map/all_gather | solution.py:155
  283.3 334.8 %all-gather.26.cloned.1.call-start = ((), (), s32[]{:S(2)}) async-start(), calls=%async_computation.12 | async-start | bytes 11943936 | tf_op jit(solution)/shard_map/all_gather | solution.py:156
  284.0 487.0 %all-gather.28.cloned.1.call-start = ((), (), s32[]{:S(2)}) async-start(), calls=%async_computation.13 | async-start | bytes 11943936 | tf_op jit(solution)/shard_map/all_gather | solution.py:157
  284.6 534.6 %reduce-scatter.7.cloned.1.call-start = ((), (), s32[]{:S(2)}) async-start(), calls=%async_computation.14 | async-start | bytes 3686400 | tf_op jit(solution)/shard_map/reduce_scatter | solution.py:236
  784.0 35.1 %copy-start.96 = (f32[2304]{0:T(1024)S(1)}, f32[2304]{0:T(1024)}, u32[]{:S(2)}) copy-start(f32[2304]{0:T(1024)} %get-tuple-element.18) | copy-start | bytes 27652
  784.1 67.1 %all-gather.30.cloned.1.call-start = ((), (), s32[]{:S(2)}) async-start(), calls=%async_computation.15 | async-start | bytes 3686400 | tf_op jit(solution)/shard_map/all_gather | solution.py:242
  823.6 119.5 %reduce-scatter.9.cloned.1.call-start = ((), (), s32[]{:S(2)}) async-start(), calls=%async_computation.16 | async-start | bytes 3686400 | tf_op jit(solution)/shard_map/reduce_scatter | solution.py:249
  871.5 15.2 %copy-start.15 = (bf16[640,2304]{1,0:T(8,128)(2,1)}, bf16[640,2304]{1,0:T(8,128)(2,1)S(1)}, u32[]{:S(2)}) copy-start(bf16[640,2304]{1,0:T(8,128)(2,1)S(1)} %get-tuple-element.46) | copy-start | bytes 8847364
  906.1 36.9 %copy-start.79 = (f32[2304]{0:T(1024)S(1)}, f32[2304]{0:T(1024)}, u32[]{:S(2)}) copy-start(f32[2304]{0:T(1024)} %copy-done.78) | copy-start | bytes 27652
  906.2 36.9 %copy-start.98 = (f32[2304]{0:T(1024)S(1)}, f32[2304]{0:T(1024)}, u32[]{:S(2)}) copy-start(f32[2304]{0:T(1024)} %get-tuple-element.19) | copy-start | bytes 27652
  906.2 36.9 %copy-start.121 = (f32[160]{0:T(256)S(1)}, f32[160]{0:T(256)}, u32[]{:S(2)}) copy-start(f32[160]{0:T(256)} %copy-done.120) | copy-start | bytes 1924
  906.2 39.0 %copy-start.130 = (f32[160]{0:T(256)S(1)}, f32[160]{0:T(256)}, u32[]{:S(2)}) copy-start(f32[160]{0:T(256)} %copy-done.129) | copy-start | bytes 1924
  906.2 39.0 %copy-start.140 = (f32[160]{0:T(256)S(1)}, f32[160]{0:T(256)}, u32[]{:S(2)}) copy-start(f32[160]{0:T(256)} %get-tuple-element.67) | copy-start | bytes 1924
  906.2 73.3 %all-gather.32.cloned.1.call-start = ((), (), s32[]{:S(2)}) async-start(), calls=%async_computation.17 | async-start | bytes 3686400 | tf_op jit(solution)/shard_map/all_gather | solution.py:254
  951.9 176.5 %all-reduce.7.cloned.1.call-start = ((), (), s32[]{:S(2)}) async-start(), calls=%async_computation.20 | async-start | bytes 4325376 | tf_op jit(solution)/shard_map/psum | solution.py:309
  952.5 34.4 %copy-start.126 = (f32[2,640]{1,0:T(2,128)}, f32[2,640]{1,0:T(2,128)S(1)}, u32[]{:S(2)}) copy-start(f32[2,640]{1,0:T(2,128)S(1)} %log_add_fusion) | copy-start | bytes 15364
  959.4 20.1 %copy-start.55 = (bf16[1,16,2304]{2,0,1:T(2,128)(2,1)S(1)}, bf16[1,16,2304]{2,0,1:T(2,128)(2,1)}, u32[]{:S(2)}) copy-start(bf16[1,16,2304]{2,0,1:T(2,128)(2,1)} %fusion.86) | copy-start | bytes 221188
  1021.9 144.6 %reduce-scatter.11.cloned.1.call-start = ((), (), s32[]{:S(2)}) async-start(), calls=%async_computation.18 | async-start | bytes 3686400 | tf_op jit(solution)/shard_map/reduce_scatter | solution.py:297
  1036.9 317.3 %all-reduce.5.cloned.1.call-start = ((), (), s32[]{:S(2)}) async-start(), calls=%async_computation.19 | async-start | bytes 16515072 | tf_op jit(solution)/shard_map/psum | solution.py:314
  1131.6 35.0 %copy-start.6 = (bf16[160,2304]{1,0:T(8,128)(2,1)S(1)}, bf16[160,2304]{1,0:T(8,128)(2,1)}, u32[]{:S(2)}) copy-start(bf16[160,2304]{1,0:T(8,128)(2,1)} %param.27) | copy-start | bytes 2211844
  1131.6 35.0 %copy-start.95 = (f32[2304]{0:T(1024)S(1)}, f32[2304]{0:T(1024)}, u32[]{:S(2)}) copy-start(f32[2304]{0:T(1024)} %copy-done.94) | copy-start | bytes 27652
  1137.0 31.0 %copy-start.18 = (f32[160,2304]{1,0:T(8,128)S(1)}, f32[160,2304]{1,0:T(8,128)}, u32[]{:S(2)}) copy-start(f32[160,2304]{1,0:T(8,128)} %copy-done.17) | copy-start | bytes 4423684
  1137.0 31.0 %copy-start.132 = (f32[160]{0:T(256)S(1)}, f32[160]{0:T(256)}, u32[]{:S(2)}) copy-start(f32[160]{0:T(256)} %copy-done.131) | copy-start | bytes 1924
  1137.0 31.0 %copy-start.139 = (f32[160]{0:T(256)S(1)}, f32[160]{0:T(256)}, u32[]{:S(2)}) copy-start(f32[160]{0:T(256)} %get-tuple-element.63) | copy-start | bytes 1924
  (110 other events, 459.9 us)
Sparse Core Ops, SparseCore 0:
  13.2 30.1 all-gather.11
  45.6 52.0 all-gather.17
  99.9 39.5 all-gather.15
  141.5 39.8 all-gather.13
  183.4 50.8 all-gather.19
  240.5 35.2 reduce-scatter.4
  282.6 27.4 all-gather.21
  312.5 152.4 all-gather.23
  467.4 150.6 all-gather.25
  620.3 150.6 all-gather.27
  784.2 34.9 reduce-scatter.6
  823.7 27.4 all-gather.29
  906.3 36.6 reduce-scatter.8
  952.0 27.4 all-gather.31
  1022.0 106.2 all-reduce.6
  1130.9 35.5 reduce-scatter.10
  1173.9 180.2 all-reduce.4
where the time goes:
time: 1380 us; the launch traced here: 1370 us
  waiting for transfers between devices  1090 us (79%)
  matrix products  187 us (14%)
  other arithmetic  55.4 us (4%)
  local copies, waits for them, and re-layouts  22.7 us (2%)
  between operations  16.2 us (1%)
    psum x1, waiting for transfers between devices, on_device(): lax.psum((hot_rows * query_back[1][None], hot_rows * key_back[1][None], h...  184 us
    all_gather x1, waiting for transfers between devices, on_device(): lax.all_gather(w_gate, 'dp', axis=0, tiled=True)  149 us
    all_gather x1, waiting for transfers between devices, on_device(): lax.all_gather(w_up, 'dp', axis=0, tiled=True)  140 us
    all_gather x1, waiting for transfers between devices, on_device(): lax.all_gather(w_down, 'dp', axis=1, tiled=True)  136 us
    psum x1, waiting for transfers between devices, on_device(): lax.psum((hot_rows * output_back[1][None]).astype(jnp.bfloat16), 'dp')  90.8 us
    dot_general x21, matrix products, product(): return jnp.dot(former, latter, preferred_element_type=jnp.float32)  83.2 us
    dot_general x7, matrix products, project_back(): jnp.einsum('lo,io->li', upstream, weight, preferred_element_type=jnp.floa...  52.5 us
    all_gather x1, waiting for transfers between devices, on_device(): lax.all_gather(w_query, 'dp', axis=0, tiled=True)  51.4 us
  transfers between devices with their start and end apart: 17, of which 17 were waited for; matrix products, arithmetic and copies ran while one was open for 8% of the time, Pallas kernels for 0%

commit v1 on v0

--- a/solution.py
+++ b/solution.py
@@ -6,6 +6,16 @@
 
 HEAD_WIDTH = 256
 ADAPTERS = 8
+
+
+def gather_by_hops(array, mesh_axis, dim):
+    size = lax.axis_size(mesh_axis)
+    block, shards = (array, [array])
+    for _ in range(size - 1):
+        block = lax.ppermute(block, mesh_axis, [(i, (i + 1) % size) for i in range(size)])
+        shards.insert(0, block)
+    line = jnp.concatenate(shards, axis=dim)
+    return jnp.roll(line, (lax.axis_index(mesh_axis) + 1) * array.shape[dim], axis=dim)
 
 
 def rms_scale(value_rows, gain_row):
@@ -239,7 +249,7 @@
     layer_output = (residual + rms_scale(ffn_out, norm_gain[3])).astype(jnp.bfloat16)
     grad_out = cotangent.astype(jnp.float32)
     grad_ffn = rms_back(ffn_out, norm_gain[3], grad_out).astype(jnp.bfloat16)
-    grad_ffn_all = lax.all_gather(grad_ffn, "tensor", axis=0, tiled=True)
+    grad_ffn_all = gather_by_hops(grad_ffn, "tensor", 0)
     down_back = project_back(hidden, down_inner, grad_ffn_all, w_down, s_down, e_down)
     grad_gate, grad_up = act_back(down_back[0])
     grad_gate = grad_gate.astype(jnp.bfloat16)

time: 1380 us -> 1390 us (level)
    ppermute x0 -> x3, waiting for transfers between devices: none -> 33.1 us  [gather_by_hops(): lax.ppermute(block, mesh_axis, [(i, (i + 1) % size) for i in range(size)])]
    all_gather x1 -> x0, waiting for transfers between devices: 27.5 us -> none  [on_device(): grad_ffn_all = lax.all_gather(grad_ffn, 'tensor', axis=0, tiled=True)]
  transfers between devices with their start and end apart: 17 -> 19, of which waited for: 17 -> 19; matrix products, arithmetic and copies ran while one was open for 8% -> 8% of each run, Pallas kernels for 0% -> 0%
where the time goes in v1:
time: 1390 us; the launch traced here: 1380 us
  waiting for transfers between devices  1090 us (78%)
  matrix products  189 us (14%)
  other arithmetic  54.4 us (4%)
  local copies, waits for them, and re-layouts  31.4 us (2%)
  between operations  16.5 us (1%)
    psum x1, waiting for transfers between devices, on_device(): lax.psum((hot_rows * query_back[1][None], hot_rows * key_back[1][None], h...  184 us
    all_gather x1, waiting for transfers between devices, on_device(): lax.all_gather(w_gate, 'dp', axis=0, tiled=True)  149 us
    all_gather x1, waiting for transfers between devices, on_device(): lax.all_gather(w_up, 'dp', axis=0, tiled=True)  140 us
    all_gather x1, waiting for transfers between devices, on_device(): lax.all_gather(w_down, 'dp', axis=1, tiled=True)  136 us
    psum x1, waiting for transfers between devices, on_device(): lax.psum((hot_rows * output_back[1][None]).astype(jnp.bfloat16), 'dp')  90.9 us
    dot_general x21, matrix products, product(): return jnp.dot(former, latter, preferred_element_type=jnp.float32)  78.6 us
    dot_general x7, matrix products, project_back(): jnp.einsum('lo,io->li', upstream, weight, preferred_element_type=jnp.floa...  58.7 us
    all_gather x1, waiting for transfers between devices, on_device(): lax.all_gather(w_query, 'dp', axis=0, tiled=True)  51.4 us
  transfers between devices with their start and end apart: 19, of which 19 were waited for; matrix products, arithmetic and copies ran while one was open for 8% of the time, Pallas kernels for 0%

profile of v1, /device:TPU:0, one launch (start us, length us, event | category | flops | bytes accessed | tf_op | source)
XLA Modules:
  0.0 1383.8 jit_solution(10951283702662141873)
XLA Ops:
  26.3 17.1 %all-gather.11.cloned.1.call-done = bf16[640,2304]{1,0:T(8,128)(2,1)} async-done(((bf16[160,2304]{1,0:T(8,128)(2,1)}), bf16[640,2304]{1,0:T(8,128)(2,1)}) %all-gather.11.cloned.1.call-update) | async-done | bytes 2949136 | tf_op jit(solution)/shard_map/all_gather | solution.py:197
  43.4 2.8 fusion.134
  46.2 51.4 %all-gather.17.cloned.1.call-done = bf16[2304,512]{1,0:T(8,128)(2,1)} async-done(((bf16[288,512]{1,0:T(8,128)(2,1)}), bf16[2304,512]{1,0:T(8,128)(2,1)}) %all-gather.17.cloned.1.call-update) | async-done | bytes 2359312 | tf_op jit(solution)/shard_map/all_gather | solution.py:161
  97.7 3.7 fusion.200
  109.0 30.5 %all-gather.15.cloned.1.call-done = bf16[2304,256]{1,0:T(8,128)(2,1)} async-done(((bf16[288,256]{1,0:T(8,128)(2,1)}), bf16[2304,256]{1,0:T(8,128)(2,1)}) %all-gather.15.cloned.1.call-update) | async-done | bytes 1179664 | tf_op jit(solution)/shard_map/all_gather | solution.py:162
  143.9 37.5 %all-gather.13.cloned.1.call-done = bf16[2304,256]{1,0:T(8,128)(2,1)} async-done(((bf16[288,256]{1,0:T(8,128)(2,1)}), bf16[2304,256]{1,0:T(8,128)(2,1)}) %all-gather.13.cloned.1.call-update) | async-done | bytes 1179664 | tf_op jit(solution)/shard_map/all_gather | solution.py:163
  190.3 44.1 %all-gather.19.cloned.1.call-done = bf16[512,2304]{0,1:T(8,128)(2,1)} async-done(((bf16[512,288]{0,1:T(8,128)(2,1)}), bf16[512,2304]{0,1:T(8,128)(2,1)}) %all-gather.19.cloned.1.call-update) | async-done | bytes 2359312 | tf_op jit(solution)/shard_map/all_gather | solution.py:164
  234.3 3.4 fusion.201
  237.7 2.6 add_convert_fusion.3
  240.4 35.4 %reduce-scatter.5.cloned.1.call-done = bf16[160,2304]{1,0:T(8,128)(2,1)} async-done(((bf16[640,2304]{1,0:T(8,128)(2,1)}), bf16[160,2304]{1,0:T(8,128)(2,1)}) %reduce-scatter.5.cloned.1.call-update) | async-done | bytes 737296 | tf_op jit(solution)/shard_map/reduce_scatter | solution.py:235
  279.9 2.5 multiply_convert_fusion.2
  287.8 22.2 %all-gather.21.cloned.1.call-done = bf16[640,2304]{1,0:T(8,128)(2,1)} async-done(((bf16[160,2304]{1,0:T(8,128)(2,1)}), bf16[640,2304]{1,0:T(8,128)(2,1)}) %all-gather.21.cloned.1.call-update) | async-done | bytes 2949136 | tf_op jit(solution)/shard_map/all_gather | solution.py:240
  310.0 3.5 fusion.139
  313.5 2.4 fusion.137
  315.9 149.0 %all-gather.23.cloned.1.call-done = bf16[2304,2304]{1,0:T(8,128)(2,1)} async-done(((bf16[288,2304]{1,0:T(8,128)(2,1)}), bf16[2304,2304]{1,0:T(8,128)(2,1)}) %all-gather.23.cloned.1.call-update) | async-done | bytes 10616848 | tf_op jit(solution)/shard_map/all_gather | solution.py:165
  464.9 9.6 fusion.202
  474.4 3.5 convolution_add_fusion.1
  478.0 140.0 %all-gather.25.cloned.1.call-done = bf16[2304,2304]{1,0:T(8,128)(2,1)} async-done(((bf16[288,2304]{1,0:T(8,128)(2,1)}), bf16[2304,2304]{1,0:T(8,128)(2,1)}) %all-gather.25.cloned.1.call-update) | async-done | bytes 10616848 | tf_op jit(solution)/shard_map/all_gather | solution.py:166
  617.9 9.5 fusion.203
  627.5 4.2 multiply_convert_fusion.1
  634.8 136.1 %all-gather.27.cloned.1.call-done = bf16[2304,2304]{0,1:T(8,128)(2,1)} async-done(((bf16[2304,288]{0,1:T(8,128)(2,1)}), bf16[2304,2304]{0,1:T(8,128)(2,1)}) %all-gather.27.cloned.1.call-update) | async-done | bytes 10616848 | tf_op jit(solution)/shard_map/all_gather | solution.py:167
  770.9 10.4 fusion.204
  781.3 2.6 add_convert_fusion.2
  783.9 35.0 %reduce-scatter.7.cloned.1.call-done = bf16[160,2304]{1,0:T(8,128)(2,1)} async-done(((bf16[640,2304]{1,0:T(8,128)(2,1)}), bf16[160,2304]{1,0:T(8,128)(2,1)}) %reduce-scatter.7.cloned.1.call-update) | async-done | bytes 737296 | tf_op jit(solution)/shard_map/reduce_scatter | solution.py:246
  823.4 10.9 collective-permute-done
  835.1 11.0 collective-permute-done.1
  846.1 11.2 collective-permute-done.2
  863.5 3.5 fusion.141
  867.0 17.6 %fusion.6 = (bf16[640,2304]{1,0:T(8,128)(2,1)}, bf16[640,2304]{1,0:T(8,128)(2,1)S(1)}) fusion(f32[640,2304]{1,0:T(8,128)S(1)} %bitcast.326, f32[640,2304]{1,0:T(8,128)} %get-tuple-element.88, f32[640,2304]{1,0:T(8,128)} %fusion.141, bf16[2304,2304]{0,1:T(8,128)(2,1)} %all-gather.27.cloned.1.call-done, bf16[1280,2304]{1,0:T(8,128)(2,1)} %copy-done.21, ...), kind=kOutput, calls=%fused_computation.8 | convolution fusion | flops 6831636480 | bytes 37158916 | tf_op jit(solution)/shard_map/lo,io->li/dot_general | solution.py:111
  889.4 12.2 fusion.206
  901.5 12.1 fusion.205
  913.7 7.3 add_convert_fusion.1
  921.3 36.7 %reduce-scatter.9.cloned.1.call-done = bf16[160,2304]{1,0:T(8,128)(2,1)} async-done(((bf16[640,2304]{1,0:T(8,128)(2,1)}), bf16[160,2304]{1,0:T(8,128)(2,1)}) %reduce-scatter.9.cloned.1.call-update) | async-done | bytes 737296 | tf_op jit(solution)/shard_map/reduce_scatter | solution.py:259
  960.1 4.2 fusion.38
  967.5 3.6 fusion.12
  976.9 17.4 %all-gather.29.cloned.1.call-done = bf16[640,2304]{1,0:T(8,128)(2,1)} async-done(((bf16[160,2304]{1,0:T(8,128)(2,1)}), bf16[640,2304]{1,0:T(8,128)(2,1)}) %all-gather.29.cloned.1.call-update) | async-done | bytes 2949136 | tf_op jit(solution)/shard_map/all_gather | solution.py:264
  994.4 2.8 fusion.135
  997.5 3.8 fusion.207
  1017.7 3.6 fusion.133
  1021.3 3.4 fusion.131
  1024.8 3.4 fusion.129
  1032.0 4.0 multiply_convert_fusion.3
  1040.8 10.2 add_convert_fusion
  1051.6 90.9 %all-reduce.7.cloned.1.call-done = (bf16[8,16,512]{2,1,0:T(8,128)(2,1)}, bf16[8,16,2304]{2,1,0:T(8,128)(2,1)}, bf16[8,16,512]{2,1,0:T(8,128)(2,1)}, bf16[8,16,25...) async-done(((bf16[8,16,512]{2,1,0:T(8,128)(2,1)}, bf16[8,16,2304]{2,1,0:T(8,128)(2,1)}, ...) | async-done | bytes 2162704 | tf_op jit(solution)/shard_map/psum | solution.py:319
  1153.3 27.3 %reduce-scatter.11.cloned.1.call-done = bf16[160,2304]{1,0:T(8,128)(2,1)} async-done(((bf16[640,2304]{1,0:T(8,128)(2,1)}), bf16[160,2304]{1,0:T(8,128)(2,1)}) %reduce-scatter.11.cloned.1.call-update) | async-done | bytes 737296 | tf_op jit(solution)/shard_map/reduce_scatter | solution.py:307
  1182.1 2.7 fusion.50
  1184.7 183.6 %all-reduce.5.cloned.1.call-done = (f32[8,16,2304]{2,1,0:T(8,128)}, f32[8,16,2304]{2,1,0:T(8,128)}, f32[8,16,2304]{2,1,0:T(8,128)}, f32[8,16,2304]{2,1,0:T(8,128...) async-done(((f32[8,16,2304]{2,1,0:T(8,128)}, f32[8,16,2304]{2,1,0:T(8,128)}, f32[8,16,2304]{2,1,0:T(8,128)}, f32[8,16,2304]{2,1,0:T(8,128)}, ...) | async-done | bytes 8257552 | tf_op jit(solution)/shard_map/psum | solution.py:324
  1368.3 2.5 copy.213
  (444 shorter events, 122.6 us)
Async XLA Ops:
  7.3 36.1 %all-gather.11.cloned.1.call-start = ((), (), s32[]{:S(2)}) async-start(), calls=%async_computation.4 | async-start | bytes 3686400 | tf_op jit(solution)/shard_map/all_gather | solution.py:197
  10.8 269.1 %copy-start.85 = (f32[2304]{0:T(1024)}, f32[2304]{0:T(1024)S(1)}, u32[]{:S(2)}) copy-start(f32[2304]{0:T(1024)S(1)} %get-tuple-element.20) | copy-start | bytes 27652
  13.1 84.6 %all-gather.17.cloned.1.call-start = ((), (), s32[]{:S(2)}) async-start(), calls=%async_computation.7 | async-start | bytes 2654208 | tf_op jit(solution)/shard_map/all_gather | solution.py:161
  13.8 125.7 %all-gather.15.cloned.1.call-start = ((), (), s32[]{:S(2)}) async-start(), calls=%async_computation.6 | async-start | bytes 1327104 | tf_op jit(solution)/shard_map/all_gather | solution.py:162
  14.6 166.8 %all-gather.13.cloned.1.call-start = ((), (), s32[]{:S(2)}) async-start(), calls=%async_computation.5 | async-start | bytes 1327104 | tf_op jit(solution)/shard_map/all_gather | solution.py:163
  15.2 219.1 %all-gather.19.cloned.1.call-start = ((), (), s32[]{:S(2)}) async-start(), calls=%async_computation.8 | async-start | bytes 2654208 | tf_op jit(solution)/shard_map/all_gather | solution.py:164
  15.7 260.1 %reduce-scatter.5.cloned.1.call-start = ((), (), s32[]{:S(2)}) async-start(), calls=%async_computation.9 | async-start | bytes 3686400 | tf_op jit(solution)/shard_map/reduce_scatter | solution.py:235
  17.1 167.0 %copy-start.117 = (f32[640]{0:T(1024)}, f32[640]{0:T(1024)S(1)}, u32[]{:S(2)}) copy-start(f32[640]{0:T(1024)S(1)} %add_convert_fusion.5) | copy-start | bytes 7684
  22.5 120.5 %copy-start.79 = (bf16[1,16,2304]{2,0,1:T(2,128)(2,1)}, bf16[1,16,2304]{2,0,1:T(2,128)(2,1)S(1)}, u32[]{:S(2)}) copy-start(bf16[1,16,2304]{2,0,1:T(2,128)(2,1)S(1)} %fusion.97) | copy-start | bytes 221188
  24.2 164.3 %copy-start.26 = (pred[640,640]{0,1:T(8,128)(4,1)}, pred[640,640]{0,1:T(8,128)(4,1)S(1)}, u32[]{:S(2)}) copy-start(pred[640,640]{0,1:T(8,128)(4,1)S(1)} %fusion.30) | copy-start | bytes 1228804
  43.4 54.3 %copy-start.2 = (bf16[640,2304]{1,0:T(8,128)(2,1)S(1)}, bf16[640,2304]{1,0:T(8,128)(2,1)}, u32[]{:S(2)}) copy-start(bf16[640,2304]{1,0:T(8,128)(2,1)} %all-gather.11.cloned.1.call-done) | copy-start | bytes 8847364
  46.2 55.2 %copy-start.97 = (bf16[640,16]{0,1:T(8,128)(2,1)}, bf16[640,16]{0,1:T(8,128)(2,1)S(1)}, u32[]{:S(2)}) copy-start(bf16[640,16]{0,1:T(8,128)(2,1)S(1)} %fusion.134) | copy-start | bytes 61444
  109.0 32.9 %copy-start.108 = (bf16[640,16]{0,1:T(8,128)(2,1)}, bf16[640,16]{0,1:T(8,128)(2,1)S(1)}, u32[]{:S(2)}) copy-start(bf16[640,16]{0,1:T(8,128)(2,1)S(1)} %fusion.132) | copy-start | bytes 61444
  143.9 39.8 %copy-start.95 = (bf16[640,16]{0,1:T(8,128)(2,1)}, bf16[640,16]{0,1:T(8,128)(2,1)S(1)}, u32[]{:S(2)}) copy-start(bf16[640,16]{0,1:T(8,128)(2,1)S(1)} %fusion.130) | copy-start | bytes 61444
  143.9 39.9 %copy-start.119 = (bf16[1,16,256]{2,0,1:T(2,128)(2,1)S(1)}, bf16[1,16,256]{2,0,1:T(2,128)(2,1)}, u32[]{:S(2)}) copy-start(bf16[1,16,256]{2,0,1:T(2,128)(2,1)} %fusion.127) | copy-start | bytes 24580
  143.9 40.2 %copy-start.138 = (f32[128]{0:T(128)S(1)}, f32[128]{0:T(128)}, u32[]{:S(2)}) copy-start(f32[128]{0:T(128)} %copy-done.137) | copy-start | bytes 1540
  190.0 47.7 %copy-start.22 = (bf16[256,2,640]{2,0,1:T(8,128)(2,1)}, bf16[256,2,640]{2,0,1:T(8,128)(2,1)S(1)}, u32[]{:S(2)}) copy-start(bf16[256,2,640]{2,0,1:T(8,128)(2,1)S(1)} %fusion.59) | copy-start | bytes 1966084
  190.2 47.5 %copy-start.106 = (bf16[640,16]{0,1:T(8,128)(2,1)}, bf16[640,16]{0,1:T(8,128)(2,1)S(1)}, u32[]{:S(2)}) copy-start(bf16[640,16]{0,1:T(8,128)(2,1)S(1)} %fusion.146) | copy-start | bytes 61444
  190.2 47.5 %copy-start.58 = (bf16[1,16,2304]{2,0,1:T(2,128)(2,1)S(1)}, bf16[1,16,2304]{2,0,1:T(2,128)(2,1)}, u32[]{:S(2)}) copy-start(bf16[1,16,2304]{2,0,1:T(2,128)(2,1)} %fusion.91) | copy-start | bytes 221188
  240.3 37.4 %copy-start.5 = (bf16[160,2304]{1,0:T(8,128)(2,1)S(1)}, bf16[160,2304]{1,0:T(8,128)(2,1)}, u32[]{:S(2)}) copy-start(bf16[160,2304]{1,0:T(8,128)(2,1)} %param.27) | copy-start | bytes 2211844
  240.3 39.5 %copy-start.102 = (f32[2304]{0:T(1024)S(1)}, f32[2304]{0:T(1024)}, u32[]{:S(2)}) copy-start(f32[2304]{0:T(1024)} %get-tuple-element.19) | copy-start | bytes 27652
  240.4 69.6 %all-gather.21.cloned.1.call-start = ((), (), s32[]{:S(2)}) async-start(), calls=%async_computation.10 | async-start | bytes 3686400 | tf_op jit(solution)/shard_map/all_gather | solution.py:240
  282.4 182.5 %all-gather.23.cloned.1.call-start = ((), (), s32[]{:S(2)}) async-start(), calls=%async_computation.11 | async-start | bytes 11943936 | tf_op jit(solution)/shard_map/all_gather | solution.py:165
  283.2 334.8 %all-gather.25.cloned.1.call-start = ((), (), s32[]{:S(2)}) async-start(), calls=%async_computation.12 | async-start | bytes 11943936 | tf_op jit(solution)/shard_map/all_gather | solution.py:166
  283.9 487.0 %all-gather.27.cloned.1.call-start = ((), (), s32[]{:S(2)}) async-start(), calls=%async_computation.13 | async-start | bytes 11943936 | tf_op jit(solution)/shard_map/all_gather | solution.py:167
  284.5 534.5 %reduce-scatter.7.cloned.1.call-start = ((), (), s32[]{:S(2)}) async-start(), calls=%async_computation.14 | async-start | bytes 3686400 | tf_op jit(solution)/shard_map/reduce_scatter | solution.py:246
  285.8 27.6 %copy-start.60 = (bf16[1,16,2304]{2,0,1:T(2,128)(2,1)}, bf16[1,16,2304]{2,0,1:T(2,128)(2,1)S(1)}, u32[]{:S(2)}) copy-start(bf16[1,16,2304]{2,0,1:T(2,128)(2,1)S(1)} %fusion.85) | copy-start | bytes 221188
  315.9 158.6 %copy-start.91 = (bf16[640,16]{0,1:T(8,128)(2,1)S(1)}, bf16[640,16]{0,1:T(8,128)(2,1)}, u32[]{:S(2)}) copy-start(bf16[640,16]{0,1:T(8,128)(2,1)} %fusion.137) | copy-start | bytes 61444
  783.9 35.1 %copy-start.101 = (f32[2304]{0:T(1024)S(1)}, f32[2304]{0:T(1024)}, u32[]{:S(2)}) copy-start(f32[2304]{0:T(1024)} %get-tuple-element.18) | copy-start | bytes 27652
  783.9 174.1 %reduce-scatter.9.cloned.1.call-start = ((), (), s32[]{:S(2)}) async-start(), calls=%async_computation.15 | async-start | bytes 3686400 | tf_op jit(solution)/shard_map/reduce_scatter | solution.py:259
  823.4 10.9 collective-permute-start
  835.1 11.0 collective-permute-start.1
  846.1 11.2 collective-permute-start.2
  921.0 36.9 %copy-start.86 = (f32[2304]{0:T(1024)S(1)}, f32[2304]{0:T(1024)}, u32[]{:S(2)}) copy-start(f32[2304]{0:T(1024)} %copy-done.85) | copy-start | bytes 27652
  921.0 36.9 %copy-start.103 = (f32[2304]{0:T(1024)S(1)}, f32[2304]{0:T(1024)}, u32[]{:S(2)}) copy-start(f32[2304]{0:T(1024)} %get-tuple-element.19) | copy-start | bytes 27652
  921.0 36.9 %copy-start.126 = (f32[160]{0:T(256)S(1)}, f32[160]{0:T(256)}, u32[]{:S(2)}) copy-start(f32[160]{0:T(256)} %copy-done.125) | copy-start | bytes 1924
  921.0 39.1 %copy-start.133 = (f32[160]{0:T(256)S(1)}, f32[160]{0:T(256)}, u32[]{:S(2)}) copy-start(f32[160]{0:T(256)} %copy-done.132) | copy-start | bytes 1924
  921.0 39.1 %copy-start.143 = (f32[160]{0:T(256)S(1)}, f32[160]{0:T(256)}, u32[]{:S(2)}) copy-start(f32[160]{0:T(256)} %get-tuple-element.67) | copy-start | bytes 1924
  921.1 73.3 %all-gather.29.cloned.1.call-start = ((), (), s32[]{:S(2)}) async-start(), calls=%async_computation.16 | async-start | bytes 3686400 | tf_op jit(solution)/shard_map/all_gather | solution.py:264
  966.8 175.6 %all-reduce.7.cloned.1.call-start = ((), (), s32[]{:S(2)}) async-start(), calls=%async_computation.19 | async-start | bytes 4325376 | tf_op jit(solution)/shard_map/psum | solution.py:319
  974.6 19.8 %copy-start.59 = (bf16[1,16,2304]{2,0,1:T(2,128)(2,1)S(1)}, bf16[1,16,2304]{2,0,1:T(2,128)(2,1)}, u32[]{:S(2)}) copy-start(bf16[1,16,2304]{2,0,1:T(2,128)(2,1)} %fusion.91) | copy-start | bytes 221188
  1036.0 144.6 %reduce-scatter.11.cloned.1.call-start = ((), (), s32[]{:S(2)}) async-start(), calls=%async_computation.17 | async-start | bytes 3686400 | tf_op jit(solution)/shard_map/reduce_scatter | solution.py:307
  1051.0 317.3 %all-reduce.5.cloned.1.call-start = ((), (), s32[]{:S(2)}) async-start(), calls=%async_computation.18 | async-start | bytes 16515072 | tf_op jit(solution)/shard_map/psum | solution.py:324
  1145.6 34.9 %copy-start.6 = (bf16[160,2304]{1,0:T(8,128)(2,1)S(1)}, bf16[160,2304]{1,0:T(8,128)(2,1)}, u32[]{:S(2)}) copy-start(bf16[160,2304]{1,0:T(8,128)(2,1)} %param.27) | copy-start | bytes 2211844
  1145.7 34.9 %copy-start.100 = (f32[2304]{0:T(1024)S(1)}, f32[2304]{0:T(1024)}, u32[]{:S(2)}) copy-start(f32[2304]{0:T(1024)} %copy-done.99) | copy-start | bytes 27652
  1151.1 31.0 %copy-start.17 = (f32[160,2304]{1,0:T(8,128)S(1)}, f32[160,2304]{1,0:T(8,128)}, u32[]{:S(2)}) copy-start(f32[160,2304]{1,0:T(8,128)} %copy-done.16) | copy-start | bytes 4423684
  1151.1 31.0 %copy-start.135 = (f32[160]{0:T(256)S(1)}, f32[160]{0:T(256)}, u32[]{:S(2)}) copy-start(f32[160]{0:T(256)} %copy-done.134) | copy-start | bytes 1924
  1151.1 31.0 %copy-start.142 = (f32[160]{0:T(256)S(1)}, f32[160]{0:T(256)}, u32[]{:S(2)}) copy-start(f32[160]{0:T(256)} %get-tuple-element.63) | copy-start | bytes 1924
  (117 other events, 518.3 us)
Sparse Core Ops, SparseCore 0:
  13.2 30.1 all-gather.10
  45.5 52.0 all-gather.16
  99.8 39.6 all-gather.14
  141.5 39.8 all-gather.12
  183.4 50.8 all-gather.18
  240.5 35.2 reduce-scatter.4
  282.5 27.4 all-gather.20
  312.4 152.4 all-gather.22
  467.3 150.6 all-gather.24
  620.2 150.6 all-gather.26
  784.0 34.9 reduce-scatter.6
  921.2 36.7 reduce-scatter.8
  966.9 27.3 all-gather.28
  1036.1 106.2 all-reduce.6
  1145.0 35.5 reduce-scatter.10
  1188.0 180.2 all-reduce.4
